TPU v7x, 512 devices: a whole 4x8x8 slice. The times are simulated.
512 devices in a mesh: cls: 64 (over x, z, y_hi), dp: 8 (over y_lo, core).
Axes of the slice: x: 4, y: 8 (y_hi: 2, y_lo: 4; y = y_hi * 4 + y_lo), z: 8, core: 2. Of those that a mesh axis runs over, the one named last changes fastest.
Arguments:
- features: bfloat16 [65536, 512], P(('cls', 'dp')), may hold values from -6 to 6
- labels: int32 [65536], P(('cls', 'dp')), may hold values from 0 to 16383, as said below
- weights: float32 [65536, 512], P('cls'), may hold values from -0.25 to 0.25
- sampled: int32 [16384], P('cls'), may hold values from 0 to 1023, as said below
Outputs:
- sample_loss: float32 [65536], P(('cls', 'dp'))
- weight_grad: float32 [16384, 512], P(('cls', 'dp'))
Inputs may be any that keep to these rules, and one draw needn't show every extreme that they name: The owner of a label is label // 256. In the rows of one device (aligned blocks of 128 rows) exactly one owner receives 4 of the labels and every other owner fewer. `sampled`: each aligned block of 256 entries holds distinct rows of the owner's bank.
All inputs are finite; a program needn't handle non-finite values.
Results may differ from a plain program's by a relative error of at most 0.0038.
Values may be sent and summed in bfloat16 or wider, within the bound.
A program may use at most 64 MiB of HBM per device.

v0:
```python
import math
import jax
import jax.numpy as jnp
from jax import lax
from jax.sharding import PartitionSpec as P

logit_scale = 64.0
margin = 0.35
epsilon = 1e-06


def normalize_rows(matrix):
    squares = jnp.sum(matrix * matrix, axis=1, keepdims=True)
    return lax.rsqrt(squares + epsilon)


def logits_of(feat_block, label_block, class_block, class_ids):
    cosine = jnp.dot(feat_block, class_block.T, preferred_element_type=jnp.float32)
    target_hit = label_block[:, None] == class_ids[None, :]
    logits = logit_scale * (cosine - margin * target_hit.astype(jnp.float32))
    return (logits, target_hit)


def per_device(features, labels, weights, sampled):
    groups = lax.axis_size("cls")
    replicas = lax.axis_size("dp")
    position = lax.axis_index("cls")
    local_rows = features.shape[0]
    feature_width = features.shape[1]
    classes = sampled.shape[0]
    capacity = local_rows // groups + 2
    feat_wide = features.astype(jnp.float32)
    unit_feats = (feat_wide * normalize_rows(feat_wide)).astype(jnp.bfloat16)
    chosen = weights[sampled]
    inverse_norm = normalize_rows(chosen)
    unit_f32 = chosen * inverse_norm
    unit_rows = unit_f32.astype(jnp.bfloat16)
    owner_ids = labels // classes
    column = labels % classes
    owner_hits = (owner_ids[:, None] == jnp.arange(groups, dtype=jnp.int32)[None, :]).astype(
        jnp.int32
    )
    earlier = jnp.cumsum(owner_hits, axis=0) - owner_hits
    ranking = jnp.sum(earlier * owner_hits, axis=1)
    buffer_slot = owner_ids * capacity + ranking
    slot_codes = jnp.arange(local_rows, dtype=jnp.int32) * classes + column
    outgoing = jnp.full((groups * capacity,), -1, jnp.int32).at[buffer_slot].set(slot_codes)
    outgoing = outgoing.reshape(groups, capacity)
    gathered = lax.all_gather(unit_feats, "cls", axis=0, tiled=True)
    group_rows = gathered.shape[0]

    def decode(incoming):
        is_valid = incoming >= 0
        safe_code = jnp.maximum(incoming, 0)
        source_row = (
            jnp.arange(incoming.shape[0], dtype=jnp.int32)[:, None] * local_rows
            + safe_code // classes
        )
        return (is_valid, source_row, safe_code % classes)

    incoming = lax.all_to_all(outgoing, "cls", split_axis=0, concat_axis=0, tiled=True)
    is_valid, source_row, class_col = decode(incoming)
    feat_rows = gathered[source_row].astype(jnp.float32)
    class_rows = unit_rows[class_col].astype(jnp.float32)
    cosine = jnp.sum(feat_rows * class_rows, axis=2)
    values = logit_scale * (cosine - margin)
    replies = lax.all_to_all(values, "cls", split_axis=0, concat_axis=0, tiled=True)
    replies, incoming = (replies, incoming)
    is_valid, source_row, class_col = decode(incoming)
    drop_index = jnp.where(is_valid, source_row, group_rows).reshape(-1)
    label_local = (
        jnp.full((group_rows,), -1, jnp.int32)
        .at[drop_index]
        .set(class_col.reshape(-1), mode="drop")
    )
    block_rows = math.gcd(group_rows, 512)
    count_blocks = group_rows // block_rows
    feat_blocks = gathered.reshape(count_blocks, block_rows, feature_width)
    label_blocks = label_local.reshape(count_blocks, block_rows)
    all_ids = jnp.arange(classes, dtype=jnp.int32)

    def first_pass(operands):
        logits, target_hit = logits_of(operands[0], operands[1], unit_rows, all_ids)
        part_sum = jnp.sum(jnp.exp(logits - logit_scale), axis=1)
        part_target = jnp.sum(jnp.where(target_hit, logits, 0.0), axis=1)
        return (part_sum, part_target)

    part_sum, part_target = lax.map(first_pass, (feat_blocks, label_blocks))
    part_sum = part_sum.reshape(group_rows)
    part_target = part_target.reshape(group_rows)
    own_start = position * local_rows
    totals = lax.psum(part_sum, "cls")
    own_target = replies.reshape(-1)[buffer_slot]
    own_total = lax.dynamic_slice_in_dim(totals, own_start, local_rows)
    sample_loss = logit_scale + jnp.log(own_total) - own_target
    total_blocks = totals.reshape(count_blocks, block_rows)
    class_ids = jnp.arange(lax.axis_size("dp") * (classes // replicas), dtype=jnp.int32)

    def accumulate(running, triple):
        logits, target_hit = logits_of(triple[0], triple[1], unit_rows, class_ids)
        softmax = jnp.exp(logits - logit_scale) / triple[2][:, None]
        grads_low = (logit_scale * (softmax - target_hit.astype(jnp.float32)) / replicas).astype(
            jnp.bfloat16
        )
        return (running + jnp.dot(grads_low.T, triple[0], preferred_element_type=jnp.float32), None)

    start_grad = jnp.zeros(
        (lax.axis_size("dp") * (classes // replicas), feature_width), jnp.float32
    )
    unit_grad, _ = lax.scan(accumulate, start_grad, (feat_blocks, label_blocks, total_blocks))
    radial = jnp.sum(unit_f32 * unit_grad, axis=1, keepdims=True)
    weight_grad = lax.psum_scatter(
        inverse_norm * (unit_grad - unit_f32 * radial), "dp", scatter_dimension=0, tiled=True
    )
    return (sample_loss, weight_grad)


def solution(mesh):
    in_specs = (P(("cls", "dp"), None), P(("cls", "dp")), P("cls", None), P("cls"))
    out_specs = (P(("cls", "dp")), P(("cls", "dp"), None))
    return jax.shard_map(
        per_device, mesh=mesh, in_specs=in_specs, out_specs=out_specs, check_vma=False
    )
```

profile of v0, /device:TPU:16, one launch (start us, length us, event | category | flops | bytes accessed | tf_op | source)
XLA Modules:
  0.0 773.6 jit_solution(14654492984104845493)
XLA Ops:
  8.4 1.7 fusion.41
  12.9 17.2 %all-to-all-start = ((s32[64,1,4]{2,1,0:T(1,128)}), s32[64,1,4]{2,1,0:T(1,128)S(1)}, u32[]{:S(2)}, u32[]{:S(2)}) async-start(s32[64,1,4]{2,1,0:T(1,128)} %bitcast.1), calls=%async_computation | async-start | bytes 65536 | tf_op jit(solution)/shard_map/all_to_all | solution.py:61
  32.8 11.6 %all-to-all-done = s32[64,1,4]{2,1,0:T(1,128)S(1)} async-done(((s32[64,1,4]{2,1,0:T(1,128)}), s32[64,1,4]{2,1,0:T(1,128)S(1)}, u32[]{:S(2)}, u32[]{:S(2)}) %all-to-all-start) | async-done | bytes 1056 | tf_op jit(solution)/shard_map/all_to_all | solution.py:61
  45.1 1.4 scatter_custom_fusion.1
  46.6 159.0 %all-gather.2.cloned.1.call-done = bf16[8192,512]{1,0:T(8,128)(2,1)} async-done(((bf16[128,512]{1,0:T(8,128)(2,1)}), bf16[8192,512]{1,0:T(8,128)(2,1)}) %all-gather.2.cloned.1.call-update) | async-done | bytes 8388624 | tf_op jit(solution)/shard_map/all_gather | solution.py:49
  205.6 44.7 %while.26 = (s32[]{:T(128)}, f32[16,512]{1,0:T(8,128)}, bf16[16,512,512]{2,1,0:T(8,128)(2,1)}, bf16[256,512]{1,0:T(8,128)(2,1)S(1)}, s32[16,512]{1,0:T(8,128)S(1)}, /*index=5*/s32[]{:T(128)}, s32[]{:T(128)}) while((s32[]{:T(128)}, f32[16,512]{1,0:T(8,128)}, bf16[16,512,512]{2,1,0:T(8,128)(2,1)}, bf16[256,512]{1,0:T(8,128)(2,1)S(1)}, ...), condition=%wide.region_8.9_spmd.clone, body=%wide.region_6.8_spmd.clone.sunk | while | flops 135003648 | bytes 798817 | solution.py:88
  213.9 1.4 fusion.63
  225.1 1.4 fusion.63
  236.3 1.4 fusion.63
  247.5 1.4 fusion.63
  251.1 435.4 %psum.7 = f32[8192]{0:T(1024)S(1)} all-reduce(f32[8192]{0:T(1024)S(1)} %bitcast.77), channel_id=1, replica_groups=mesh['cls'=64,'dp'=8] {'cls'}, use_global_device_ids=true, to_apply=%region_9.10 | all-reduce | flops 8192 | bytes 65536 | tf_op jit(solution)/shard_map/psum | solution.py:92
  686.5 47.0 %while.27 = (s32[]{:T(128)}, f32[256,512]{1,0:T(8,128)S(1)}, bf16[16,512,512]{2,1,0:T(8,128)(2,1)}, bf16[256,512]{1,0:T(8,128)(2,1)S(1)}, s32[16,512]{1,0:T(8,12...) while((s32[]{:T(128)}, f32[256,512]{1,0:T(8,128)S(1)}, bf16[16,512,512]{2,1,0:T(8,128)(2,1)}, ...), condition=%wide.region_12.13_spmd.clone, body=%wide.region_11.12_spmd.clone.sunk | while | flops 270008320 | bytes 2373230 | solution.py:110
  687.2 2.1 convolution_add_fusion.2
  690.1 2.1 convolution_add_fusion.2
  693.1 2.1 convolution_add_fusion.2
  696.0 2.2 convolution_add_fusion.2
  698.9 2.1 convolution_add_fusion.2
  701.9 2.2 convolution_add_fusion.2
  704.8 2.1 convolution_add_fusion.2
  707.7 2.1 convolution_add_fusion.2
  710.7 2.1 convolution_add_fusion.2
  713.6 2.2 convolution_add_fusion.2
  716.5 2.1 convolution_add_fusion.2
  719.4 2.2 convolution_add_fusion.2
  722.4 2.2 convolution_add_fusion.2
  725.3 2.3 convolution_add_fusion.2
  728.4 2.2 convolution_add_fusion.2
  731.3 2.1 convolution_add_fusion.2
  734.3 1.7 subtract_multiply_fusion
  738.1 5.7 gather_fusion.1
  744.7 4.6 all-to-all-start.1
  749.4 14.2 %all-to-all-done.1 = f32[64,1,4]{2,1,0:T(1,128)S(1)} async-done(((f32[64,1,4]{2,1,0:T(1,128)}), f32[64,1,4]{2,1,0:T(1,128)S(1)}, u32[]{:S(2)}, u32[]{:S(2)}) %all-to-all-start.1) | async-done | bytes 1056 | tf_op jit(solution)/shard_map/all_to_all | solution.py:67
  (144 shorter events, 65.7 us)
Async XLA Ops:
  7.2 23.7 %copy-start = (f32[1024,512]{1,0:T(8,128)S(1)}, f32[1024,512]{1,0:T(8,128)}, u32[]{:S(2)}) copy-start(f32[1024,512]{1,0:T(8,128)} %param.10) | copy-start | bytes 6291460
  7.2 198.4 %all-gather.2.cloned.1.call-start = ((), (), s32[]{:S(2)}) async-start(), calls=%async_computation.3 | async-start | bytes 8519680 | tf_op jit(solution)/shard_map/all_gather | solution.py:49
  11.2 19.0 %copy-start.4 = (s32[128]{0:T(128)}, s32[128]{0:T(128)S(1)}, u32[]{:S(2)}) copy-start(s32[128]{0:T(128)S(1)} %compare_select_fusion.4) | copy-start | bytes 1540
  12.9 31.5 %all-to-all-start = ((s32[64,1,4]{2,1,0:T(1,128)}), s32[64,1,4]{2,1,0:T(1,128)S(1)}, u32[]{:S(2)}, u32[]{:S(2)}) async-start(s32[64,1,4]{2,1,0:T(1,128)} %bitcast.1), calls=%async_computation | async-start | bytes 65536 | tf_op jit(solution)/shard_map/all_to_all | solution.py:61
  30.2 736.6 %reduce-scatter.2.cloned.1.call-start = ((), (), s32[]{:S(2)}) async-start(), calls=%async_computation.4 | async-start | bytes 589824 | tf_op jit(solution)/shard_map/reduce_scatter | solution.py:112
  32.0 0.6 copy-start.2
  32.1 12.4 %copy-start.3 = (s32[64]{0:T(128)}, s32[64]{0:T(128)S(1)}, u32[]{:S(2)}) copy-start(s32[64]{0:T(128)S(1)} %iota_multiply_fusion) | copy-start | bytes 772
  250.3 0.8 copy-start.1
  733.5 15.9 %copy-start.5 = (s32[128]{0:T(128)S(1)}, s32[128]{0:T(128)}, u32[]{:S(2)}) copy-start(s32[128]{0:T(128)} %copy-done.4) | copy-start | bytes 1540
  744.7 18.9 %all-to-all-start.1 = ((f32[64,1,4]{2,1,0:T(1,128)}), f32[64,1,4]{2,1,0:T(1,128)S(1)}, u32[]{:S(2)}, u32[]{:S(2)}) async-start(f32[64,1,4]{2,1,0:T(1,128)} %bitcast.10), calls=%async_computation.1 | async-start | bytes 65536 | tf_op jit(solution)/shard_map/all_to_all | solution.py:67
Sparse Core Ops, SparseCore 0:
  12.5 193.0 all-gather.1
  736.2 23.3 reduce-scatter.1
where the time goes:
time: 777 us; the launch traced here: 774 us
  blocking collectives  435 us (56%)
  waiting for transfers between devices  185 us (24%)
  matrix products  57.7 us (7%)
  local copies, waits for them, and re-layouts  49.1 us (6%)
  starting transfers between devices  21.9 us (3%)
  between operations  14.4 us (2%)
  other arithmetic  9.74 us (1%)
    psum x1, blocking collectives, per_device(): totals = lax.psum(part_sum, 'cls')  435 us
    all_gather x1, waiting for transfers between devices, per_device(): gathered = lax.all_gather(unit_feats, 'cls', axis=0, tiled=True)  159 us
    dot_general x16, matrix products, accumulate(): jnp.dot(grads_low.T, triple[0], preferred_element_type=jnp.float32)  34.6 us
    dot_general x16, matrix products, logits_of(): jnp.dot(feat_block, class_block.T, preferred_element_type=jnp.float32)  23 us
    dynamic_update_slice x16, local copies, waits for them, and re-layouts, per_device(): part_sum, part_target = lax.map(first_pass, (feat_blocks, label_blocks))  21.5 us
    all_to_all x1, starting transfers between devices, per_device(): lax.all_to_all(outgoing, 'cls', split_axis=0, concat_axis=0, tiled=True)  17.2 us
  transfers between devices with their start and end apart: 4, of which 3 were waited for; matrix products, arithmetic and copies ran while one was open for 2% of the time, Pallas kernels for 0%

commit v1 on v0

--- a/solution.py
+++ b/solution.py
@@ -46,7 +46,9 @@
     slot_codes = jnp.arange(local_rows, dtype=jnp.int32) * classes + column
     outgoing = jnp.full((groups * capacity,), -1, jnp.int32).at[buffer_slot].set(slot_codes)
     outgoing = outgoing.reshape(groups, capacity)
-    gathered = lax.all_gather(unit_feats, "cls", axis=0, tiled=True)
+    gathered = jnp.concatenate(
+        lax.all_to_all(jnp.stack([unit_feats] * lax.axis_size("cls")), "cls", 0, 0), axis=0
+    )
     group_rows = gathered.shape[0]
 
     def decode(incoming):

time: 777 us -> 846 us (1.089)
  the two profiles are of different devices: /device:TPU:16 before, /device:TPU:8 now
where the time goes in v1:
time: 846 us; the launch traced here: 842 us
  blocking collectives  429 us (51%)
  waiting for transfers between devices  249 us (29%)
  matrix products  57.7 us (7%)
  local copies, waits for them, and re-layouts  53.9 us (6%)
  starting transfers between devices  28.7 us (3%)
  between operations  14.4 us (2%)
    psum x1, blocking collectives, per_device(): totals = lax.psum(part_sum, 'cls')  429 us
    all_to_all x1, waiting for transfers between devices, per_device(): lax.all_to_all(jnp.stack([unit_feats] * lax.axis_size('cls')), 'cls', 0, 0)  223 us
    dot_general x16, matrix products, accumulate(): jnp.dot(grads_low.T, triple[0], preferred_element_type=jnp.float32)  34.6 us
    dot_general x16, matrix products, logits_of(): jnp.dot(feat_block, class_block.T, preferred_element_type=jnp.float32)  23 us
    dynamic_update_slice x16, local copies, waits for them, and re-layouts, per_device(): part_sum, part_target = lax.map(first_pass, (feat_blocks, label_blocks))  21.5 us
    all_to_all x1, starting transfers between devices, per_device(): lax.all_to_all(outgoing, 'cls', split_axis=0, concat_axis=0, tiled=True)  18.1 us
  transfers between devices with their start and end apart: 4, of which 3 were waited for; matrix products, arithmetic and copies ran while one was open for 2% of the time, Pallas kernels for 0%

profile of v1, /device:TPU:8, one launch (start us, length us, event | category | flops | bytes accessed | tf_op | source)
XLA Modules:
  0.0 842.3 jit_solution(18249755262208067773)
XLA Ops:
  10.2 18.1 %all-to-all-start.1 = ((s32[64,1,4]{2,1,0:T(1,128)}), s32[64,1,4]{2,1,0:T(1,128)S(1)}, u32[]{:S(2)}, u32[]{:S(2)}) async-start(s32[64,1,4]{2,1,0:T(1,128)} %bitcast.1), calls=%async_computation.1 | async-start | bytes 65536 | tf_op jit(solution)/shard_map/all_to_all | solution.py:63
  30.4 12.1 %all-to-all-done.1 = s32[64,1,4]{2,1,0:T(1,128)S(1)} async-done(((s32[64,1,4]{2,1,0:T(1,128)}), s32[64,1,4]{2,1,0:T(1,128)S(1)}, u32[]{:S(2)}, u32[]{:S(2)}) %all-to-all-start.1) | async-done | bytes 1056 | tf_op jit(solution)/shard_map/all_to_all | solution.py:63
  42.5 4.2 stack.2
  46.7 5.9 all-to-all-start
  55.3 1.4 scatter_custom_fusion.1
  56.8 222.9 %all-to-all-done = bf16[64,128,512]{2,1,0:T(8,128)(2,1)} async-done(((bf16[64,128,512]{2,1,0:T(8,128)(2,1)}), bf16[64,128,512]{2,1,0:T(8,128)(2,1)}, u32[]{:S(2)}, u32[]{:S(2)}) %all-to-all-start) | async-done | bytes 8388640 | tf_op jit(solution)/shard_map/all_to_all | solution.py:50
  279.7 44.7 %while.26 = (s32[]{:T(128)}, f32[16,512]{1,0:T(8,128)}, bf16[16,512,512]{2,1,0:T(8,128)(2,1)}, bf16[256,512]{1,0:T(8,128)(2,1)S(1)}, s32[16,512]{1,0:T(8,128)S(1)}, /*index=5*/s32[]{:T(128)}, s32[]{:T(128)}) while((s32[]{:T(128)}, f32[16,512]{1,0:T(8,128)}, bf16[16,512,512]{2,1,0:T(8,128)(2,1)}, bf16[256,512]{1,0:T(8,128)(2,1)S(1)}, ...), condition=%wide.region_8.9_spmd.clone, body=%wide.region_6.8_spmd.clone.sunk | while | flops 135003648 | bytes 799317 | solution.py:90
  290.9 1.4 fusion.63
  302.1 1.4 fusion.63
  313.3 1.4 fusion.63
  325.8 429.2 %psum.7 = f32[8192]{0:T(1024)S(1)} all-reduce(f32[8192]{0:T(1024)S(1)} %bitcast.74), channel_id=1, replica_groups=mesh['cls'=64,'dp'=8] {'cls'}, use_global_device_ids=true, to_apply=%region_9.10 | all-reduce | flops 8192 | bytes 65536 | tf_op jit(solution)/shard_map/psum | solution.py:94
  755.0 46.9 %while.27 = (s32[]{:T(128)}, f32[256,512]{1,0:T(8,128)S(1)}, bf16[16,512,512]{2,1,0:T(8,128)(2,1)}, bf16[256,512]{1,0:T(8,128)(2,1)S(1)}, s32[16,512]{1,0:T(8,12...) while((s32[]{:T(128)}, f32[256,512]{1,0:T(8,128)S(1)}, bf16[16,512,512]{2,1,0:T(8,128)(2,1)}, ...), condition=%wide.region_12.13_spmd.clone, body=%wide.region_11.12_spmd.clone.sunk | while | flops 270008320 | bytes 2372711 | solution.py:112
  755.8 2.1 convolution_add_fusion.2
  758.7 2.1 convolution_add_fusion.2
  761.6 2.1 convolution_add_fusion.2
  764.5 2.2 convolution_add_fusion.2
  767.5 2.1 convolution_add_fusion.2
  770.4 2.2 convolution_add_fusion.2
  773.3 2.1 convolution_add_fusion.2
  776.3 2.1 convolution_add_fusion.2
  779.2 2.1 convolution_add_fusion.2
  782.1 2.2 convolution_add_fusion.2
  785.0 2.1 convolution_add_fusion.2
  787.9 2.2 convolution_add_fusion.2
  790.9 2.2 convolution_add_fusion.2
  793.8 2.3 convolution_add_fusion.2
  796.9 2.2 convolution_add_fusion.2
  799.8 2.1 convolution_add_fusion.2
  802.9 1.7 subtract_multiply_fusion
  806.7 5.7 gather_fusion.1
  813.3 4.6 all-to-all-start.2
  817.9 14.3 %all-to-all-done.2 = f32[64,1,4]{2,1,0:T(1,128)S(1)} async-done(((f32[64,1,4]{2,1,0:T(1,128)}), f32[64,1,4]{2,1,0:T(1,128)S(1)}, u32[]{:S(2)}, u32[]{:S(2)}) %all-to-all-start.2) | async-done | bytes 1056 | tf_op jit(solution)/shard_map/all_to_all | solution.py:69
  (146 shorter events, 68.1 us)
Async XLA Ops:
  7.2 45.8 %copy-start = (f32[1024,512]{1,0:T(8,128)S(1)}, f32[1024,512]{1,0:T(8,128)}, u32[]{:S(2)}) copy-start(f32[1024,512]{1,0:T(8,128)} %param.10) | copy-start | bytes 6291460
  8.4 20.9 %copy-start.5 = (s32[128]{0:T(128)}, s32[128]{0:T(128)S(1)}, u32[]{:S(2)}) copy-start(s32[128]{0:T(128)S(1)} %compare_select_fusion.4) | copy-start | bytes 1540
  10.2 32.3 %all-to-all-start.1 = ((s32[64,1,4]{2,1,0:T(1,128)}), s32[64,1,4]{2,1,0:T(1,128)S(1)}, u32[]{:S(2)}, u32[]{:S(2)}) async-start(s32[64,1,4]{2,1,0:T(1,128)} %bitcast.1), calls=%async_computation.1 | async-start | bytes 65536 | tf_op jit(solution)/shard_map/all_to_all | solution.py:63
  46.7 6.2 copy-start.4
  46.7 233.0 %all-to-all-start = ((bf16[64,128,512]{2,1,0:T(8,128)(2,1)}), bf16[64,128,512]{2,1,0:T(8,128)(2,1)}, u32[]{:S(2)}, u32[]{:S(2)}) async-start(bf16[64,128,512]{2,1,0:T(8,128)(2,1)} %stack.2), calls=%async_computation | async-start | bytes 16777216 | tf_op jit(solution)/shard_map/all_to_all | solution.py:50
  52.6 782.8 %reduce-scatter.2.cloned.1.call-start = ((), (), s32[]{:S(2)}) async-start(), calls=%async_computation.4 | async-start | bytes 589824 | tf_op jit(solution)/shard_map/reduce_scatter | solution.py:114
  52.7 1.3 copy-start.3
  54.0 0.6 copy-start.2
  324.4 0.6 copy-start.1
  802.0 15.9 %copy-start.6 = (s32[128]{0:T(128)S(1)}, s32[128]{0:T(128)}, u32[]{:S(2)}) copy-start(s32[128]{0:T(128)} %copy-done.5) | copy-start | bytes 1540
  813.3 18.9 %all-to-all-start.2 = ((f32[64,1,4]{2,1,0:T(1,128)}), f32[64,1,4]{2,1,0:T(1,128)S(1)}, u32[]{:S(2)}, u32[]{:S(2)}) async-start(f32[64,1,4]{2,1,0:T(1,128)} %bitcast.11), calls=%async_computation.2 | async-start | bytes 65536 | tf_op jit(solution)/shard_map/all_to_all | solution.py:69
Sparse Core Ops, SparseCore 0:
  804.7 25.0 reduce-scatter.1
